TPU v7x, 32 devices: a whole 2x2x4 slice. The times are simulated.
32 devices in a mesh: ka: 16 (over z, y, core), aux: 2 (over x).
Axes of the slice: x: 2, y: 2, z: 4, core: 2. Of those that a mesh axis runs over, the one named last changes fastest.
Arguments:
- coefficients: bfloat16 [16, 4096, 128], P('ka'), may hold values from -2.09375 to 2.09375
- triple: bfloat16 [64, 2, 64, 768], P('aux'), may hold values from -0.5 to 0.5
- neighbors: int32 [64, 2], P('aux'), may hold values from 0 to 63
- w_screened: bfloat16 [16, 768, 1536], P('ka', 'aux'), as said below
- partner: int32 [2, 16], replicated, may hold values from 0 to 15, each once within a row
- q_ids: int32 [2], replicated, may hold values from 0 to 15
Outputs:
- sigma: float32 [16, 64, 128], P('ka', 'aux')
Inputs may be any that keep to these rules, and one draw needn't show every extreme that they name: Each stored w_screened is Hermitian: its real block is symmetric and its imaginary block antisymmetric.
All inputs are finite; a program needn't handle non-finite values.
Results may differ from a plain program's by a relative error of at most 0.0085.
Values may be sent and summed in bfloat16 or wider, within the bound.
A program may use at most 128 MiB of HBM per device.

v0:
```python
import math
import jax
import jax.numpy as jnp
from jax import lax
from jax.sharding import PartitionSpec as P

CELL_ATOMS = 64
ORBITALS_PER_ATOM = 64
AUX_ATOM = 12
OCCUPIED_BANDS = 16
TRANSFERS = 2
NAUX = 768


def from_root(block, axis, source):
    block = jnp.where(lax.axis_index(axis) == source, block, jnp.zeros_like(block))
    return lax.psum(block, axis)


def from_partner(value, axis, distance):
    mask = 2**distance
    pairs = [(source, source ^ mask) for source in range(lax.axis_size(axis))]
    return lax.ppermute(value, axis, pairs)


def rotated_parts(values, band_count):
    return jnp.concatenate([-values[..., band_count:], values[..., :band_count]], axis=-1)


def apply_block(weights, start, values, band_count):
    kpoints, rows, occupied, doubled = values.shape
    real_cols = lax.dynamic_slice_in_dim(weights, start, rows, 1)
    imag_cols = lax.dynamic_slice_in_dim(weights, NAUX + start, rows, 1)
    flat = values.reshape(kpoints, rows, occupied * doubled)
    turned = rotated_parts(values, band_count).reshape(kpoints, rows, occupied * doubled)
    result = jnp.einsum("ab,kbx->kax", real_cols, flat, preferred_element_type=jnp.float32)
    result = result + jnp.einsum(
        "ab,kbx->kax", imag_cols, turned, preferred_element_type=jnp.float32
    )
    return result.reshape(kpoints, weights.shape[0], occupied, doubled)


def pair_blocks(left_values, right_values):
    kpoints = left_values.shape[0]
    doubled = left_values.shape[-1]
    left_flat = left_values.reshape(kpoints, -1, doubled)
    right_flat = right_values.reshape(kpoints, -1, doubled)
    return jnp.einsum("kxm,kxn->kmn", left_flat, right_flat, preferred_element_type=jnp.float32)


def sigma_parts(blocks, band_count):
    sigma_real = blocks[:, :band_count, :band_count] + blocks[:, band_count:, band_count:]
    sigma_imag = blocks[:, :band_count, band_count:] - blocks[:, band_count:, :band_count]
    return (sigma_real, sigma_imag)


def local(coefficients, triple, neighbors, w_screened, partner, q_ids):
    kpoints, orbitals, doubled = coefficients.shape
    band_count = doubled // 2
    local_atoms = triple.shape[0]
    local_aux = local_atoms * AUX_ATOM
    half_index = lax.axis_index("aux")
    prefactor = -1.0 / math.sqrt(TRANSFERS * NAUX * OCCUPIED_BANDS)
    screens = [
        from_root(w_screened[0], "ka", q_ids[momentum_transfer])
        for momentum_transfer in range(TRANSFERS)
    ]
    far_cols = jnp.concatenate(
        [
            coefficients[:, :, :OCCUPIED_BANDS],
            coefficients[:, :, band_count : band_count + OCCUPIED_BANDS],
        ],
        axis=2,
    )
    packed = far_cols.reshape(kpoints, orbitals * 2 * OCCUPIED_BANDS // 128, 128)
    spread = lax.all_to_all(packed, "ka", split_axis=1, concat_axis=0, tiled=True)
    permuted = jnp.take(spread, partner, axis=0)
    arrived = jnp.stack(
        [
            lax.all_to_all(
                permuted[momentum_transfer], "ka", split_axis=0, concat_axis=1, tiled=True
            )
            for momentum_transfer in range(TRANSFERS)
        ]
    )
    distant_coefficients = arrived.reshape(
        TRANSFERS, kpoints, CELL_ATOMS, ORBITALS_PER_ATOM, 2 * OCCUPIED_BANDS
    )
    own_rows = lax.dynamic_slice_in_dim(
        coefficients,
        half_index * local_atoms * ORBITALS_PER_ATOM,
        local_atoms * ORBITALS_PER_ATOM,
        1,
    )
    home_coefficients = own_rows.reshape(kpoints, local_atoms, ORBITALS_PER_ATOM, doubled)
    neighbour_coef = jnp.take(distant_coefficients, neighbors, axis=2)
    pair_half = jnp.einsum(
        "tkcjoy,cjox->tkcyx", neighbour_coef, triple, preferred_element_type=jnp.float32
    ).astype(jnp.bfloat16)
    pair_half = pair_half.reshape(
        TRANSFERS, kpoints, local_atoms, 2 * OCCUPIED_BANDS, AUX_ATOM, ORBITALS_PER_ATOM
    )
    combos = jnp.einsum(
        "kcix,tkcyai->tkcayx", home_coefficients, pair_half, preferred_element_type=jnp.float32
    )
    real_part = (
        combos[..., :OCCUPIED_BANDS, :band_count] + combos[..., OCCUPIED_BANDS:, band_count:]
    )
    imag_part = (
        combos[..., OCCUPIED_BANDS:, :band_count] - combos[..., :OCCUPIED_BANDS, band_count:]
    )
    products = jnp.concatenate([real_part, imag_part], axis=-1).astype(jnp.bfloat16)
    products = products.reshape(TRANSFERS, kpoints, local_aux, OCCUPIED_BANDS, doubled)
    pairs = products.reshape(TRANSFERS // 2, 2, kpoints, local_aux, OCCUPIED_BANDS, doubled)
    screen_pairs = jnp.stack(screens).reshape(TRANSFERS // 2, 2, local_aux, 2 * NAUX)
    outgoing = lax.dynamic_index_in_dim(pairs, 1 - half_index, 1, keepdims=False)
    incoming = from_partner(outgoing, "aux", 0)
    own_start = half_index * local_aux
    other_start = (1 - half_index) * local_aux
    full_weights = lax.dynamic_index_in_dim(screen_pairs[0], half_index, 0, keepdims=False)
    part_weights = lax.dynamic_index_in_dim(screen_pairs[0], 1 - half_index, 0, keepdims=False)
    full_values = lax.dynamic_index_in_dim(pairs[0], half_index, 0, keepdims=False)
    part_values = lax.dynamic_index_in_dim(pairs[0], 1 - half_index, 0, keepdims=False)
    cross = apply_block(full_weights, other_start, incoming[0], band_count)
    full_screened = (apply_block(full_weights, own_start, full_values, band_count) + cross).astype(
        jnp.bfloat16
    )
    part_screened = apply_block(part_weights, own_start, part_values, band_count).astype(
        jnp.bfloat16
    )
    cross_screened = cross.astype(jnp.bfloat16)
    diagonal = pair_blocks(full_values, full_screened) + pair_blocks(part_values, part_screened)
    diag_real, diag_imag = sigma_parts(diagonal, band_count)
    cross_real, cross_imag = sigma_parts(pair_blocks(full_values, cross_screened), band_count)
    total_real = diag_real + jnp.transpose(cross_real, (0, 2, 1))
    total_imag = diag_imag - jnp.transpose(cross_imag, (0, 2, 1))
    local_sigma = jnp.concatenate([total_real, total_imag], axis=-1)
    local_sigma = prefactor * local_sigma
    return lax.psum_scatter(
        local_sigma.astype(jnp.bfloat16), "aux", scatter_dimension=1, tiled=True
    ).astype(jnp.float32)


def solution(mesh):
    in_specs = (
        P("ka", None, None),
        P("aux", None, None, None),
        P("aux", None),
        P("ka", "aux", None),
        P(),
        P(),
    )
    out_specs = P("ka", "aux", None)
    return jax.shard_map(local, mesh=mesh, in_specs=in_specs, out_specs=out_specs, check_vma=False)
```

profile of v0, /device:TPU:0, one launch (start us, length us, event | category | flops | bytes accessed | tf_op | source)
XLA Modules:
  0.0 210.7 jit_solution(5651449956877544662)
XLA Ops:
  13.9 7.4 %all-to-all-start = ((bf16[16,2,4096]{2,1,0:T(2,128)(2,1)}), bf16[16,2,4096]{2,1,0:T(2,128)(2,1)S(1)}, u32[]{:S(2)}, u32[]{:S(2)}) async-start(bf16[16,2,4096]{2,1,0:T(2,128)(2,1)} %reshape.297), calls=%async_computation | async-start | bytes 524288 | tf_op jit(solution)/shard_map/all_to_all | solution.py:76
  23.3 8.0 %all-to-all-done = bf16[16,2,4096]{2,1,0:T(2,128)(2,1)S(1)} async-done(((bf16[16,2,4096]{2,1,0:T(2,128)(2,1)}), bf16[16,2,4096]{2,1,0:T(2,128)(2,1)S(1)}, u32[]{:S(2)}, u32[]{:S(2)}) %all-to-all-start) | async-done | bytes 262176 | tf_op jit(solution)/shard_map/all_to_all | solution.py:76
  33.3 3.5 %all-to-all-start.1 = ((bf16[16,64,128]{2,1,0:T(8,128)(2,1)}), bf16[16,64,128]{2,1,0:T(8,128)(2,1)S(1)}, u32[]{:S(2)}, u32[]{:S(2)}) async-start(bf16[16,64,128]{2,1,0:T(8,128)(2,1)} %get-tuple-element.21), calls=%async_computation.1 | async-start | bytes 524288 | tf_op jit(solution)/shard_map/all_to_all | solution.py:80
  39.3 7.4 %all-to-all-done.1 = bf16[16,64,128]{2,1,0:T(8,128)(2,1)S(1)} async-done(((bf16[16,64,128]{2,1,0:T(8,128)(2,1)}), bf16[16,64,128]{2,1,0:T(8,128)(2,1)S(1)}, u32[]{:S(2)}, u32[]{:S(2)}) %all-to-all-start.1) | async-done | bytes 262176 | tf_op jit(solution)/shard_map/all_to_all | solution.py:80
  46.8 3.5 %all-to-all-start.2 = ((bf16[16,64,128]{2,1,0:T(8,128)(2,1)}), bf16[16,64,128]{2,1,0:T(8,128)(2,1)S(1)}, u32[]{:S(2)}, u32[]{:S(2)}) async-start(bf16[16,64,128]{2,1,0:T(8,128)(2,1)} %get-tuple-element.22), calls=%async_computation.2 | async-start | bytes 524288 | tf_op jit(solution)/shard_map/all_to_all | solution.py:80
  52.0 11.2 %all-to-all-done.2 = bf16[16,64,128]{2,1,0:T(8,128)(2,1)S(1)} async-done(((bf16[16,64,128]{2,1,0:T(8,128)(2,1)}), bf16[16,64,128]{2,1,0:T(8,128)(2,1)S(1)}, u32[]{:S(2)}, u32[]{:S(2)}) %all-to-all-start.2) | async-done | bytes 262176 | tf_op jit(solution)/shard_map/all_to_all | solution.py:80
  68.4 2.8 %copy.46 = bf16[64,2,64,32]{2,3,1,0:T(8,128)(2,1)} copy(bf16[64,2,64,32]{3,2,1,0:T(8,128)(2,1)} %gather_fusion.1) | data formatting | bytes 1048576 | tf_op jit(solution)/shard_map/jit(_take)/gather | solution.py:96
  71.1 4.9 %fusion.9 = bf16[2,1,32,32,768]{4,3,0,2,1:T(8,128)(2,1)S(1)} fusion(bf16[32,2,64,768]{3,2,1,0:T(8,128)(2,1)} %param.7, bf16[32,2,2,64,32]{3,4,2,1,0:T(8,128)(2,1)} %bitcast.155, pred[32,2]{1,0:T(8,128)(4,1)S(1)} %copy.40), kind=kOutput, calls=%fused_computation.12 | convolution fusion | flops 404488192 | bytes 9961536 | tf_op jit(solution)/shard_map/tkcjoy,cjox->tkcyx/dot_general | solution.py:97
  76.0 7.2 %reshape.296 = bf16[2,32,32,12,64]{4,3,2,0,1:T(8,128)(2,1)} reshape(bf16[2,1,32,32,768]{4,3,0,2,1:T(8,128)(2,1)S(1)} %fusion.9) | data formatting | bytes 6291456 | tf_op jit(solution)/shard_map/reshape.12
  83.2 5.1 %fusion.6 = f32[2,1,32,12,32,128]{5,4,3,0,2,1:T(8,128)S(1)} fusion(bf16[32,64,128,1,1]{2,1,4,3,0:T(8,128)(2,1)} %bitcast.160, bf16[2,32,32,12,64]{4,3,2,0,1:T(8,128)(2,1)} %reshape.296), kind=kOutput, calls=%fused_computation.11 | convolution fusion | flops 402653184 | bytes 16252928 | tf_op jit(solution)/shard_map/kcix,tkcyai->tkcayx/dot_general | solution.py:103
  88.3 3.7 %fusion = (bf16[2,1,32,12,16,64]{5,4,3,0,2,1:T(8,128)(2,1)S(1)}, bf16[2,1,32,12,16,64]{5,4,3,0,2,1:T(8,128)(2,1)S(1)}) fusion(f32[2,1,32,12,32,128]{5,4,3,0,2,1:T(8,128)S(1)} %fusion.6), kind=kLoop, calls=%fused_computation.3 | loop fusion | flops 3145728 | bytes 15728640 | tf_op jit(solution)/shard_map/convert.6
  104.1 42.1 %all-reduce.3.cloned.1.call-done = (bf16[1,384,1536]{2,1,0:T(8,128)(2,1)}, bf16[1,384,1536]{2,1,0:T(8,128)(2,1)}) async-done(((bf16[1,384,1536]{2,1,0:T(8,128)(2,1)}, bf16[1,384,1536]{2,1,0:T(8,128)(2,1)}), (bf16[1,384,1536]{2,1,0:T(8,128)(2,1)}, bf16[1,384,1536]{2,1,0:T(8,128)(2,1)})) %all-reduce.3.cloned.1.call-update) | async-done | bytes 2359312 | tf_op jit(solution)/shard_map/psum | solution.py:17
  150.2 2.5 %fusion.11 = bf16[1,384,2048]{1,2,0:T(8,128)(2,1)} fusion(f32[2048,384]{1,0:T(8,128)S(1)} %fusion.20, bf16[48,8,16,128]{3,2,1,0:T(8,128)(2,1)S(1)} %bitcast.157, bf16[2,384,1536]{2,1,0:T(8,128)(2,1)S(1)} %constant_dynamic-update-slice_fusion, s32[]{:T(128)S(6)} %select_n.104, s32[]{:T(128)S(6)} %select_n.98), kind=kOutput, calls=%fused_computation.23 | convolution fusion | flops 605552640 | bytes 6586376 | tf_op jit(solution)/shard_map/ab,kbx->kax/dot_general | solution.py:37
  152.7 2.6 %copy.55 = bf16[1,384,2048]{2,1,0:T(8,128)(2,1)} copy(bf16[1,384,2048]{1,2,0:T(8,128)(2,1)} %fusion.11) | data formatting | bytes 3145728 | tf_op jit(solution)/shard_map/convert_element_type | solution.py:128
  155.3 3.7 %convert_element_type.101 = bf16[6144,128]{1,0:T(8,128)(2,1)} reshape(bf16[1,384,2048]{2,1,0:T(8,128)(2,1)} %copy.55) | data formatting | bytes 3145728 | tf_op jit(solution)/shard_map/convert_element_type | solution.py:128
  159.1 2.3 %fusion.30 = f32[2048,384]{1,0:T(8,128)S(1)} fusion(bf16[48,8,16,128]{3,2,1,0:T(8,128)(2,1)S(1)} %bitcast.144, bf16[2,384,1536]{2,1,0:T(8,128)(2,1)} %copy-done.5, s32[]{:T(128)S(6)} %select_n.94, s32[]{:T(128)S(6)} %select_n.96), kind=kOutput, calls=%fused_computation.41 | convolution fusion | flops 603979776 | bytes 5013512 | tf_op jit(solution)/shard_map/ab,kbx->kax/dot_general | solution.py:36
  161.3 2.6 %slice_negate_fusion.1 = (bf16[1,384,16,64]{3,2,1,0:T(8,128)(2,1)S(1)}, bf16[1,384,16,64]{3,2,1,0:T(8,128)(2,1)S(1)}) fusion(bf16[1,384,16,128]{3,2,1,0:T(8,128)(2,1)} %bitcast.31), kind=kLoop, calls=%fused_computation.45 | loop fusion | flops 393216 | bytes 3145728 | tf_op jit(solution)/shard_map/neg | solution.py:27
  167.0 2.8 %convolution_add_fusion = f32[2048,384]{1,0:T(8,128)S(1)} fusion(f32[2048,384]{1,0:T(8,128)S(1)} %fusion.23, bf16[48,8,16,128]{3,2,1,0:T(8,128)(2,1)} %bitcast.70, bf16[2,384,1536]{2,1,0:T(8,128)(2,1)} %copy-done.5, s32[]{:T(128)S(6)} %select_n.94, s32[]{:T(128)S(6)} %select_n.101), kind=kOutput, calls=%fused_computation.17 | convolution fusion | flops 604766208 | bytes 8159240 | tf_op jit(solution)/shard_map/ab,kbx->kax/dot_general | solution.py:36
  171.8 3.6 %fusion.10 = bf16[1,384,2048]{1,2,0:T(8,128)(2,1)} fusion(f32[2048,384]{1,0:T(8,128)S(1)} %convolution_add_fusion, f32[2048,384]{1,0:T(8,128)S(1)} %fusion.30, bf16[48,8,16,128]{3,2,1,0:T(8,128)(2,1)S(1)} %bitcast.156, bf16[2,384,1536]{2,1,0:T(8,128)(2,1)} %copy-done.5, s32[]{:T(128)S(6)} %select_n.94, s32[]{:T(128)S(6)} %select_n.98), kind=kOutput, calls=%fused_computation.22 | convolution fusion | flops 606339072 | bytes 9732104 | tf_op jit(solution)/shard_map/ab,kbx->kax/dot_general | solution.py:37
  175.4 2.7 %copy.54 = bf16[1,384,2048]{2,1,0:T(8,128)(2,1)} copy(bf16[1,384,2048]{1,2,0:T(8,128)(2,1)} %fusion.10) | data formatting | bytes 3145728 | tf_op jit(solution)/shard_map/convert_element_type | solution.py:125
  178.1 3.7 %convert_element_type.97 = bf16[6144,128]{1,0:T(8,128)(2,1)} reshape(bf16[1,384,2048]{2,1,0:T(8,128)(2,1)} %copy.54) | data formatting | bytes 3145728 | tf_op jit(solution)/shard_map/convert_element_type | solution.py:125
  181.8 2.6 %copy.56 = bf16[1,384,2048]{2,1,0:T(8,128)(2,1)} copy(bf16[1,384,2048]{1,2,0:T(8,128)(2,1)} %convert_bitcast_fusion) | data formatting | bytes 3145728 | tf_op jit(solution)/shard_map/convert_element_type | solution.py:131
  184.4 3.7 %convert_element_type.105 = bf16[6144,128]{1,0:T(8,128)(2,1)} reshape(bf16[1,384,2048]{2,1,0:T(8,128)(2,1)} %copy.56) | data formatting | bytes 3145728 | tf_op jit(solution)/shard_map/convert_element_type | solution.py:131
  193.2 9.4 %reduce-scatter.2.cloned.1.call-done = bf16[1,32,128]{2,1,0:T(8,128)(2,1)} async-done(((bf16[1,64,128]{2,1,0:T(8,128)(2,1)}), bf16[1,32,128]{2,1,0:T(8,128)(2,1)}) %reduce-scatter.2.cloned.1.call-update) | async-done | bytes 8208 | tf_op jit(solution)/shard_map/reduce_scatter | solution.py:139
  (79 shorter events, 46.5 us)
Async XLA Ops:
  9.7 11.6 %copy-start.9 = (s32[2,16]{1,0:T(2,128)S(1)}, s32[2,16]{1,0:T(2,128)}, u32[]{:S(2)}) copy-start(s32[2,16]{1,0:T(2,128)} %param.10) | copy-start | bytes 388
  9.8 11.7 %copy-start.8 = (s32[2]{0:T(128)S(1)}, s32[2]{0:T(128)}, u32[]{:S(2)}) copy-start(s32[2]{0:T(128)} %param.11) | copy-start | bytes 28
  13.9 17.4 %all-to-all-start = ((bf16[16,2,4096]{2,1,0:T(2,128)(2,1)}), bf16[16,2,4096]{2,1,0:T(2,128)(2,1)S(1)}, u32[]{:S(2)}, u32[]{:S(2)}) async-start(bf16[16,2,4096]{2,1,0:T(2,128)(2,1)} %reshape.297), calls=%async_computation | async-start | bytes 524288 | tf_op jit(solution)/shard_map/all_to_all | solution.py:76
  32.3 4.6 %copy-start.7 = (bf16[1,384,1536]{2,1,0:T(8,128)(2,1)S(1)}, bf16[1,384,1536]{2,1,0:T(8,128)(2,1)}, u32[]{:S(2)}) copy-start(bf16[1,384,1536]{2,1,0:T(8,128)(2,1)} %param.9) | copy-start | bytes 3538948
  33.3 13.5 %all-to-all-start.1 = ((bf16[16,64,128]{2,1,0:T(8,128)(2,1)}), bf16[16,64,128]{2,1,0:T(8,128)(2,1)S(1)}, u32[]{:S(2)}, u32[]{:S(2)}) async-start(bf16[16,64,128]{2,1,0:T(8,128)(2,1)} %get-tuple-element.21), calls=%async_computation.1 | async-start | bytes 524288 | tf_op jit(solution)/shard_map/all_to_all | solution.py:80
  36.8 109.4 %all-reduce.3.cloned.1.call-start = ((), (), s32[]{:S(2)}) async-start(), calls=%async_computation.5 | async-start | bytes 4718592 | tf_op jit(solution)/shard_map/psum | solution.py:17
  38.5 0.7 copy-start.10
  38.5 12.2 %copy-start = (bf16[1,4096,128]{2,1,0:T(8,128)(2,1)S(1)}, bf16[1,4096,128]{2,1,0:T(8,128)(2,1)}, u32[]{:S(2)}) copy-start(bf16[1,4096,128]{2,1,0:T(8,128)(2,1)} %param.6) | copy-start | bytes 3145732
  46.8 16.4 %all-to-all-start.2 = ((bf16[16,64,128]{2,1,0:T(8,128)(2,1)}), bf16[16,64,128]{2,1,0:T(8,128)(2,1)S(1)}, u32[]{:S(2)}, u32[]{:S(2)}) async-start(bf16[16,64,128]{2,1,0:T(8,128)(2,1)} %get-tuple-element.22), calls=%async_computation.2 | async-start | bytes 524288 | tf_op jit(solution)/shard_map/all_to_all | solution.py:80
  50.3 152.2 %reduce-scatter.2.cloned.1.call-start = ((), (), s32[]{:S(2)}) async-start(), calls=%async_computation.4 | async-start | bytes 24576 | tf_op jit(solution)/shard_map/reduce_scatter | solution.py:139
  95.4 65.9 %collective-permute-start = (bf16[1,1,384,16,128]{4,3,2,1,0:T(8,128)(2,1)}, bf16[1,1,384,16,128]{4,3,2,1,0:T(8,128)(2,1)}, u32[]{:S(2)}, u32[]{:S(2)}) collective-permute-start(bf16[1,1,384,16,128]{4,3,2,1,0:T(8,128)(2,1)} %fusion.17), channel_id=1, source_target_pairs={{0,1},{1,0},{2,3},{3,2},{4,5},{5,4},{6,7},{7,6},{8,9},{9,8},{10,11... | collective-permute-start | bytes 4718600 | tf_op jit(solution)/shard_map/ppermute | solution.py:23
  146.2 1.6 copy-start.6
  147.9 1.4 copy-start.5
  147.9 2.3 %copy-start.4 = (bf16[1,384,16,128]{3,2,1,0:T(8,128)(2,1)S(1)}, bf16[1,384,16,128]{3,2,1,0:T(8,128)(2,1)}, u32[]{:S(2)}) copy-start(bf16[1,384,16,128]{3,2,1,0:T(8,128)(2,1)} %pad_maximum_fusion.2) | copy-start | bytes 4718596
  169.8 2.0 copy-start.1
  188.2 2.1 %copy-start.3 = (bf16[6144,128]{1,0:T(8,128)(2,1)S(1)}, bf16[6144,128]{1,0:T(8,128)(2,1)}, u32[]{:S(2)}) copy-start(bf16[6144,128]{1,0:T(8,128)(2,1)} %convert_element_type.105) | copy-start | bytes 4718596
  190.3 1.4 copy-start.2
Sparse Core Ops, SparseCore 0:
  41.2 104.9 all-reduce.2
  193.3 9.2 reduce-scatter.1
where the time goes:
time: 212 us; the launch traced here: 211 us
  waiting for transfers between devices  78.2 us (37%)
  local copies, waits for them, and re-layouts  47.6 us (22%)
  matrix products  28.1 us (13%)
  other arithmetic  25.5 us (12%)
  starting transfers between devices  16.3 us (8%)
  between operations  15.1 us (7%)
    psum x1, waiting for transfers between devices, from_root(): return lax.psum(block, axis)  42.1 us
    all_to_all x2, waiting for transfers between devices, local(): lax.all_to_all(permuted[momentum_transfer], 'ka', split_axis=0, concat_ax...  18.6 us
    reduce_scatter x1, waiting for transfers between devices, local(): lax.psum_scatter(local_sigma.astype(jnp.bfloat16), 'aux', scatter_dimensi...  9.4 us
    another operation x3, local copies, waits for them, and re-layouts  8.42 us
    dot_general x3, matrix products, apply_block(): jnp.einsum('ab,kbx->kax', imag_cols, turned, preferred_element_type=jnp.f...  8.36 us
    all_to_all x1, waiting for transfers between devices, local(): lax.all_to_all(packed, 'ka', split_axis=1, concat_axis=0, tiled=True)  8.01 us
    all_to_all x1, starting transfers between devices, local(): lax.all_to_all(packed, 'ka', split_axis=1, concat_axis=0, tiled=True)  7.41 us
    all_to_all x2, starting transfers between devices, local(): lax.all_to_all(permuted[momentum_transfer], 'ka', split_axis=0, concat_ax...  7.06 us
  transfers between devices with their start and end apart: 6, of which 5 were waited for; matrix products, arithmetic and copies ran while one was open for 27% of the time, Pallas kernels for 0%

commit v1 on v0

--- a/solution.py
+++ b/solution.py
@@ -14,7 +14,7 @@
 
 def from_root(block, axis, source):
     block = jnp.where(lax.axis_index(axis) == source, block, jnp.zeros_like(block))
-    return lax.psum(block, axis)
+    return jnp.sum(jax.lax.all_gather(block, axis_name=axis), axis=0)
 
 
 def from_partner(value, axis, distance):

time: 212 us -> 299 us (1.41)
  waiting for transfers between devices: 78.2 us -> 145 us
  other arithmetic: 25.5 us -> 51 us
    all_gather x0 -> x2, waiting for transfers between devices: none -> 67.7 us  [from_root(): return jnp.sum(jax.lax.all_gather(block, axis_name=axis), axis=0)]
    psum x1 -> x0, waiting for transfers between devices: 42.1 us -> none  [from_root(): return lax.psum(block, axis)]
    ppermute x1, waiting for transfers between devices: 0.01 us -> 24.7 us  [from_partner(): return lax.ppermute(value, axis, pairs)]
    reduce_sum x0 -> x2, other arithmetic: none -> 22.2 us  [from_root(): return jnp.sum(jax.lax.all_gather(block, axis_name=axis), axis=0)]
    all_to_all x2, waiting for transfers between devices: 18.6 us -> 27.4 us  [local(): lax.all_to_all(permuted[momentum_transfer], 'ka', split_axis=0, concat_ax...]
    all_to_all x1, waiting for transfers between devices: 8.01 us -> 14.5 us  [local(): lax.all_to_all(packed, 'ka', split_axis=1, concat_axis=0, tiled=True)]
    unnamed x29 -> x42, local copies, waits for them, and re-layouts: 6.87 us -> 7.49 us
    another operation x4 -> x3, local copies, waits for them, and re-layouts: 8.49 us -> 8.19 us
  transfers between devices with their start and end apart: 6 -> 7, of which waited for: 5 -> 6; matrix products, arithmetic and copies ran while one was open for 27% -> 22% of each run, Pallas kernels for 0% -> 0%
where the time goes in v1:
time: 299 us; the launch traced here: 298 us
  waiting for transfers between devices  145 us (48%)
  other arithmetic  51 us (17%)
  local copies, waits for them, and re-layouts  44.9 us (15%)
  matrix products  25.9 us (9%)
  starting transfers between devices  16.2 us (5%)
  between operations  14.7 us (5%)
    all_gather x2, waiting for transfers between devices, from_root(): return jnp.sum(jax.lax.all_gather(block, axis_name=axis), axis=0)  67.7 us
    all_to_all x2, waiting for transfers between devices, local(): lax.all_to_all(permuted[momentum_transfer], 'ka', split_axis=0, concat_ax...  27.4 us
    ppermute x1, waiting for transfers between devices, from_partner(): return lax.ppermute(value, axis, pairs)  24.7 us
    reduce_sum x2, other arithmetic, from_root(): return jnp.sum(jax.lax.all_gather(block, axis_name=axis), axis=0)  22.2 us
    all_to_all x1, waiting for transfers between devices, local(): lax.all_to_all(packed, 'ka', split_axis=1, concat_axis=0, tiled=True)  14.5 us
    reduce_scatter x1, waiting for transfers between devices, local(): lax.psum_scatter(local_sigma.astype(jnp.bfloat16), 'aux', scatter_dimensi...  9.93 us
    another operation x3, local copies, waits for them, and re-layouts  8.19 us
    unnamed x42, local copies, waits for them, and re-layouts  7.49 us
  transfers between devices with their start and end apart: 7, of which 6 were waited for; matrix products, arithmetic and copies ran while one was open for 22% of the time, Pallas kernels for 0%

profile of v1, /device:TPU:0, one launch (start us, length us, event | category | flops | bytes accessed | tf_op | source)
XLA Modules:
  0.0 297.7 jit_solution(99819223803620270)
XLA Ops:
  9.1 2.9 broadcast_select_fusion
  18.9 7.4 %all-to-all-start = ((bf16[16,2,4096]{2,1,0:T(2,128)(2,1)}), bf16[16,2,4096]{2,1,0:T(2,128)(2,1)S(1)}, u32[]{:S(2)}, u32[]{:S(2)}) async-start(bf16[16,2,4096]{2,1,0:T(2,128)(2,1)} %reshape.289), calls=%async_computation | async-start | bytes 524288 | tf_op jit(solution)/shard_map/all_to_all | solution.py:76
  26.4 14.5 %all-to-all-done = bf16[16,2,4096]{2,1,0:T(2,128)(2,1)S(1)} async-done(((bf16[16,2,4096]{2,1,0:T(2,128)(2,1)}), bf16[16,2,4096]{2,1,0:T(2,128)(2,1)S(1)}, u32[]{:S(2)}, u32[]{:S(2)}) %all-to-all-start) | async-done | bytes 262176 | tf_op jit(solution)/shard_map/all_to_all | solution.py:76
  42.9 3.5 %all-to-all-start.2 = ((bf16[16,64,128]{2,1,0:T(8,128)(2,1)}), bf16[16,64,128]{2,1,0:T(8,128)(2,1)S(1)}, u32[]{:S(2)}, u32[]{:S(2)}) async-start(bf16[16,64,128]{2,1,0:T(8,128)(2,1)} %get-tuple-element.20), calls=%async_computation.2 | async-start | bytes 524288 | tf_op jit(solution)/shard_map/all_to_all | solution.py:80
  46.6 14.5 %all-to-all-done.2 = bf16[16,64,128]{2,1,0:T(8,128)(2,1)S(1)} async-done(((bf16[16,64,128]{2,1,0:T(8,128)(2,1)}), bf16[16,64,128]{2,1,0:T(8,128)(2,1)S(1)}, u32[]{:S(2)}, u32[]{:S(2)}) %all-to-all-start.2) | async-done | bytes 262176 | tf_op jit(solution)/shard_map/all_to_all | solution.py:80
  61.0 3.5 %all-to-all-start.1 = ((bf16[16,64,128]{2,1,0:T(8,128)(2,1)}), bf16[16,64,128]{2,1,0:T(8,128)(2,1)S(1)}, u32[]{:S(2)}, u32[]{:S(2)}) async-start(bf16[16,64,128]{2,1,0:T(8,128)(2,1)} %get-tuple-element.19), calls=%async_computation.1 | async-start | bytes 524288 | tf_op jit(solution)/shard_map/all_to_all | solution.py:80
  66.3 12.9 %all-to-all-done.1 = bf16[16,64,128]{2,1,0:T(8,128)(2,1)S(1)} async-done(((bf16[16,64,128]{2,1,0:T(8,128)(2,1)}), bf16[16,64,128]{2,1,0:T(8,128)(2,1)S(1)}, u32[]{:S(2)}, u32[]{:S(2)}) %all-to-all-start.1) | async-done | bytes 262176 | tf_op jit(solution)/shard_map/all_to_all | solution.py:80
  84.4 2.7 copy.46
  87.1 5.0 %fusion.9 = bf16[2,1,32,32,768]{4,3,0,2,1:T(8,128)(2,1)S(1)} fusion(bf16[32,2,64,768]{3,2,1,0:T(8,128)(2,1)} %param.7, bf16[32,2,2,64,32]{3,4,2,1,0:T(8,128)(2,1)} %bitcast.170, pred[32,2]{1,0:T(8,128)(4,1)S(1)} %copy.40), kind=kOutput, calls=%fused_computation.24 | convolution fusion | flops 404488192 | bytes 9961536 | tf_op jit(solution)/shard_map/tkcjoy,cjox->tkcyx/dot_general | solution.py:97
  92.1 7.1 %reshape.288 = bf16[2,32,32,12,64]{4,3,2,0,1:T(8,128)(2,1)} reshape(bf16[2,1,32,32,768]{4,3,0,2,1:T(8,128)(2,1)S(1)} %fusion.9) | data formatting | bytes 6291456 | tf_op jit(solution)/shard_map/reshape.12
  99.2 5.3 %fusion.6 = f32[2,1,32,12,32,128]{5,4,3,0,2,1:T(8,128)S(1)} fusion(bf16[32,64,128,1,1]{2,1,4,3,0:T(8,128)(2,1)} %bitcast.176, bf16[2,32,32,12,64]{4,3,2,0,1:T(8,128)(2,1)} %reshape.288), kind=kOutput, calls=%fused_computation.11 | convolution fusion | flops 402653184 | bytes 16252928 | tf_op jit(solution)/shard_map/kcix,tkcyai->tkcayx/dot_general | solution.py:103
  104.5 3.7 %fusion = (bf16[2,1,32,12,16,64]{5,4,3,0,2,1:T(8,128)(2,1)S(1)}, bf16[2,1,32,12,16,64]{5,4,3,0,2,1:T(8,128)(2,1)S(1)}) fusion(f32[2,1,32,12,32,128]{5,4,3,0,2,1:T(8,128)S(1)} %fusion.6), kind=kLoop, calls=%fused_computation.3 | loop fusion | flops 3145728 | bytes 15728640 | tf_op jit(solution)/shard_map/convert.8
  114.0 4.6 %fusion.14 = (bf16[1,1,384,16,128]{4,3,2,0,1:T(8,128)(2,1)S(1)}, bf16[1,1,384,16,128]{4,3,2,0,1:T(8,128)(2,1)S(1)}) fusion(s32[]{:T(128)S(6)} %select_n.93, bf16[2,1,384,16,64]{4,3,2,0,1:T(8,128)(2,1)} %bitcast.167, bf16[2,1,384,16,64]{4,3,2,0,1:T(8,128)(2,1)} %bitcast.165, s32[]{:T(128)S(6)} %select_n.83), kind=kLoop, calls=%fused_computation.37 | loop fusion | flops 6291456 | bytes 6291464 | tf_op jit(solution)/shard_map/concatenate | solution.py:112
  124.0 24.7 %collective-permute-done = bf16[1,1,384,16,128]{4,3,2,1,0:T(8,128)(2,1)S(1)} collective-permute-done((bf16[1,1,384,16,128]{4,3,2,1,0:T(8,128)(2,1)}, bf16[1,1,384,16,128]{4,3,2,1,0:T(8,128)(2,1)S(1)}, u32[]{:S(2)}, u32[]{:S(2)}) %collective-permute-start) | collective-permute-done | bytes 1572896 | tf_op jit(solution)/shard_map/ppermute | solution.py:23
  151.9 10.6 %reduce_sum.25 = bf16[384,1536]{1,0:T(8,128)(2,1)S(1)} reduce(bf16[16,384,1536]{2,1,0:T(8,128)(2,1)} %all-gather.5.cloned.1.call-done, bf16[]{:T(256)} %constant.170.clone.1), dimensions={0}, to_apply=%region_1.2 | reduce | flops 8847360 | bytes 20054018 | tf_op jit(solution)/shard_map/reduce_sum | solution.py:17
  162.5 67.7 %all-gather.3.cloned.1.call-done = bf16[16,384,1536]{2,1,0:T(8,128)(2,1)} async-done(((bf16[1,384,1536]{2,1,0:T(8,128)(2,1)}), bf16[16,384,1536]{2,1,0:T(8,128)(2,1)}) %all-gather.3.cloned.1.call-update) | async-done | bytes 18874384 | tf_op jit(solution)/shard_map/all_gather | solution.py:17
  230.2 11.6 %reduce_sum.24 = bf16[384,1536]{1,0:T(8,128)(2,1)} reduce(bf16[16,384,1536]{2,1,0:T(8,128)(2,1)} %all-gather.3.cloned.1.call-done, bf16[]{:T(256)} %constant.170.clone.1), dimensions={0}, to_apply=%region_0.1 | reduce | flops 8847360 | bytes 20054018 | tf_op jit(solution)/shard_map/reduce_sum | solution.py:17
  241.8 2.9 fusion.23
  249.1 2.6 copy.56
  251.7 3.8 %convert_element_type.109 = bf16[6144,128]{1,0:T(8,128)(2,1)} reshape(bf16[1,384,2048]{2,1,0:T(8,128)(2,1)} %copy.56) | data formatting | bytes 3145728 | tf_op jit(solution)/shard_map/convert_element_type | solution.py:131
  258.3 2.7 fusion.10
  263.6 3.7 %convert_element_type.101 = bf16[6144,128]{1,0:T(8,128)(2,1)} reshape(bf16[1,384,2048]{2,1,0:T(8,128)(2,1)} %copy.54) | data formatting | bytes 3145728 | tf_op jit(solution)/shard_map/convert_element_type | solution.py:125
  275.8 2.7 convert_element_type.105
  280.0 9.9 %reduce-scatter.2.cloned.1.call-done = bf16[1,32,128]{2,1,0:T(8,128)(2,1)} async-done(((bf16[1,64,128]{2,1,0:T(8,128)(2,1)}), bf16[1,32,128]{2,1,0:T(8,128)(2,1)}) %reduce-scatter.2.cloned.1.call-update) | async-done | bytes 8208 | tf_op jit(solution)/shard_map/reduce_scatter | solution.py:139
  (96 shorter events, 52.3 us)
Async XLA Ops:
  6.5 145.3 %all-gather.5.cloned.1.call-start = ((), (), s32[]{:S(2)}) async-start(), calls=%async_computation.5 | async-start | bytes 20054016 | tf_op jit(solution)/shard_map/all_gather | solution.py:17
  12.0 1.2 copy-start.12
  12.0 218.2 %all-gather.3.cloned.1.call-start = ((), (), s32[]{:S(2)}) async-start(), calls=%async_computation.4 | async-start | bytes 20054016 | tf_op jit(solution)/shard_map/all_gather | solution.py:17
  14.7 11.6 %copy-start.16 = (s32[2,16]{1,0:T(2,128)S(1)}, s32[2,16]{1,0:T(2,128)}, u32[]{:S(2)}) copy-start(s32[2,16]{1,0:T(2,128)} %param.10) | copy-start | bytes 388
  18.9 22.1 %all-to-all-start = ((bf16[16,2,4096]{2,1,0:T(2,128)(2,1)}), bf16[16,2,4096]{2,1,0:T(2,128)(2,1)S(1)}, u32[]{:S(2)}, u32[]{:S(2)}) async-start(bf16[16,2,4096]{2,1,0:T(2,128)(2,1)} %reshape.289), calls=%async_computation | async-start | bytes 524288 | tf_op jit(solution)/shard_map/all_to_all | solution.py:76
  41.9 4.5 %copy-start.17 = (s32[32,2]{0,1:T(2,128)S(1)}, s32[32,2]{0,1:T(2,128)}, u32[]{:S(2)}) copy-start(s32[32,2]{0,1:T(2,128)} %param.8) | copy-start | bytes 772
  42.9 18.2 %all-to-all-start.2 = ((bf16[16,64,128]{2,1,0:T(8,128)(2,1)}), bf16[16,64,128]{2,1,0:T(8,128)(2,1)S(1)}, u32[]{:S(2)}, u32[]{:S(2)}) async-start(bf16[16,64,128]{2,1,0:T(8,128)(2,1)} %get-tuple-element.20), calls=%async_computation.2 | async-start | bytes 524288 | tf_op jit(solution)/shard_map/all_to_all | solution.py:80
  61.0 18.2 %all-to-all-start.1 = ((bf16[16,64,128]{2,1,0:T(8,128)(2,1)}), bf16[16,64,128]{2,1,0:T(8,128)(2,1)S(1)}, u32[]{:S(2)}, u32[]{:S(2)}) async-start(bf16[16,64,128]{2,1,0:T(8,128)(2,1)} %get-tuple-element.19), calls=%async_computation.1 | async-start | bytes 524288 | tf_op jit(solution)/shard_map/all_to_all | solution.py:80
  64.6 225.3 %reduce-scatter.2.cloned.1.call-start = ((), (), s32[]{:S(2)}) async-start(), calls=%async_computation.6 | async-start | bytes 24576 | tf_op jit(solution)/shard_map/reduce_scatter | solution.py:139
  108.8 1.7 copy-start.8
  109.3 3.1 %copy-start.9 = (bf16[2,1,32,12,16,64]{5,4,3,2,0,1:T(8,128)(2,1)}, bf16[2,1,32,12,16,64]{5,4,3,2,0,1:T(8,128)(2,1)S(1)}, u32[]{:S(2)}) copy-start(bf16[2,1,32,12,16,64]{5,4,3,2,0,1:T(8,128)(2,1)S(1)} %copy.50) | copy-start | bytes 4718596
  112.5 36.2 %collective-permute-start = (bf16[1,1,384,16,128]{4,3,2,1,0:T(8,128)(2,1)}, bf16[1,1,384,16,128]{4,3,2,1,0:T(8,128)(2,1)S(1)}, u32[]{:S(2)}, u32[]{:S(2)}) collective-permute-start(bf16[1,1,384,16,128]{4,3,2,1,0:T(8,128)(2,1)} %fusion.17), channel_id=1, source_target_pairs={{0,1},{1,0},{2,3},{3,2},{4,5},{5,4},{6,7},{7,6},{8,9},{9,8},{10,11... | collective-permute-start | bytes 4718600 | tf_op jit(solution)/shard_map/ppermute | solution.py:23
  118.6 2.7 copy-start.3
  241.8 2.9 copy-start
  241.8 2.9 copy-start.11
  246.1 1.6 copy-start.6
  255.5 2.5 copy-start.1
  255.5 2.5 copy-start.7
  255.5 2.8 copy-start.14
  267.4 2.1 copy-start.15
  269.5 1.3 copy-start.2
  269.5 1.8 copy-start.4
  271.3 1.4 copy-start.13
  275.8 2.7 copy-start.5
  (1 other events, 1.2 us)
Sparse Core Ops, SparseCore 0:
  12.1 114.2 all-gather.4
  128.0 102.1 all-gather.2
  280.1 9.7 reduce-scatter.1
